TPU v7x, 32 devices: a whole 2x2x4 slice. The times are simulated.
32 devices in a mesh: seq: 4 (over y, x), head: 8 (over z, core).
Axes of the slice: x: 2, y: 2, z: 4, core: 2. Of those that a mesh axis runs over, the one named last changes fastest.
Arguments:
- inputs: bfloat16 [4096, 6144], P('seq', 'head'), may hold values from -6 to 6
- projection: bfloat16 [6144, 3, 4096], P('seq', None, 'head'), may hold values from -0.078125 to 0.078125
- cotangent: bfloat16 [4096, 4096], P('seq', 'head'), may hold values from -0.3125 to 0.3125
- log_decay: float32 [32, 4096], P('head', 'seq'), may hold values from -0.7 to 0
- document_starts: int32 [4], replicated, may hold values from 0 to 3328, as said below
Outputs:
- input_gradient: bfloat16 [4096, 6144], P('seq', 'head')
- weight_gradient: bfloat16 [6144, 3, 4096], P('seq', None, 'head')
Inputs may be any that keep to these rules, and one draw needn't show every extreme that they name: `document_starts`: strictly increasing; the first is 0 and the last is (3) * 1024 + 256.
All inputs are finite; a program needn't handle non-finite values.
Results may differ from a plain program's by a relative error of at most 0.02.
Values may be sent and summed in bfloat16 or wider, within the bound.
A program may use at most 192 MiB of HBM per device.

v0:
```python
import jax
import jax.numpy as jnp
from jax import lax
from jax.sharding import PartitionSpec as P

HEAD_DIM = 128
BLOCK = 256


def prefix(array, axis, combine, identity, reverse):
    length, place = (lax.axis_size(axis), lax.axis_index(axis))
    everything = jax.tree.map(
        lambda part, kind: lax.all_gather(part.astype(kind), axis),
        array,
        (jnp.bfloat16, jnp.bfloat16),
    )
    start = jax.tree.map(
        lambda part, zero: jnp.broadcast_to(jnp.asarray(zero, part.dtype), part.shape),
        array,
        identity,
    )

    def turn(k, before):
        at = length - 1 - k if reverse else k
        reached = at > place if reverse else at < place
        new = combine(
            before, jax.tree.map(lambda part, own: part[at].astype(own.dtype), everything, array)
        )
        return jax.tree.map(lambda a, b: jnp.where(reached, a, b), new, before)

    return lax.fori_loop(0, length, turn, start)


def silu_slope(point):
    sigma = jax.nn.sigmoid(point)
    return sigma * (1.0 + point * (1.0 - sigma))


def block_factors(decay_sum, doc_index, doc_begin):
    inside = jnp.arange(doc_index.shape[-1], dtype=jnp.int32)
    causal = inside[:, None] >= inside[None, :]
    same_doc = (doc_index[:, :, None] == doc_index[:, None, :]) & causal[None]
    spread = jnp.minimum(decay_sum[..., :, None] - decay_sum[..., None, :], 0.0)
    pair_weight = jnp.where(same_doc[None], jnp.exp(spread), 0.0)
    to_end = jnp.where(
        (doc_index == doc_index[:, -1:])[None], jnp.exp(decay_sum[..., -1:] - decay_sum), 0.0
    )
    began_flag = doc_index == doc_index[:, :1] - doc_begin[:, :1]
    from_start = jnp.where(began_flag[None], jnp.exp(decay_sum), 0.0)
    return (pair_weight, to_end, from_start, from_start[..., -1])


def combine_states(earlier, later):
    return (earlier[0] * later[0], later[0][:, None, None] * earlier[1] + later[1])


def body(inputs, projection, cotangent, log_decay, document_starts):
    tokens = inputs.shape[0]
    heads_here = log_decay.shape[0]
    local_cols = cotangent.shape[1]
    blocks = tokens // BLOCK
    query_scale = HEAD_DIM ** (-0.5)
    features = lax.all_gather(inputs, "head", axis=1, tiled=True)
    weights_all = lax.all_gather(projection, "seq", axis=0, tiled=True)
    projected = jnp.einsum("td,dkc->tkc", features, weights_all, preferred_element_type=jnp.float32)
    queries = (jax.nn.silu(projected[:, 0]) * query_scale).astype(jnp.bfloat16)
    keys = jax.nn.silu(projected[:, 1]).astype(jnp.bfloat16)
    values = projected[:, 2].astype(jnp.bfloat16)

    def split_blocks(table):
        return table.reshape(blocks, BLOCK, heads_here, HEAD_DIM).transpose(2, 0, 1, 3)

    def merge_blocks(table):
        return table.transpose(1, 2, 0, 3).reshape(tokens, local_cols)

    queries_b = split_blocks(queries)
    keys_b = split_blocks(keys)
    values_b = split_blocks(values)
    upstream = split_blocks(cotangent)
    offset = lax.axis_index("seq") * tokens
    positions = offset + jnp.arange(tokens, dtype=jnp.int32)
    doc_index = (
        jnp.sum((document_starts[None, :] <= positions[:, None]).astype(jnp.int32), axis=1) - 1
    )
    doc_begin = jnp.any(document_starts[None, :] == positions[:, None], axis=1).astype(jnp.int32)
    decay_sum = jnp.cumsum(log_decay.reshape(heads_here, blocks, BLOCK), axis=-1)
    pair_weight, to_end, from_start, block_decay = block_factors(
        decay_sum, doc_index.reshape(blocks, BLOCK), doc_begin.reshape(blocks, BLOCK)
    )
    keys_weighted = (keys_b.astype(jnp.float32) * to_end[..., None]).astype(jnp.bfloat16)
    queries_weighted = (queries_b.astype(jnp.float32) * from_start[..., None]).astype(jnp.bfloat16)
    key_state = jnp.einsum(
        "hbse,hbsf->hbef", keys_weighted, values_b, preferred_element_type=jnp.float32
    )
    query_state = jnp.einsum(
        "hbte,hbtf->hbef", queries_weighted, upstream, preferred_element_type=jnp.float32
    )

    def local_step(carry, item):
        return (combine_states(carry, item), carry)

    ones = jnp.ones((heads_here,), jnp.float32)
    empty = jnp.zeros((heads_here, HEAD_DIM, HEAD_DIM), jnp.float32)
    (device_decay, device_keys), (prior_decay, prior_keys) = lax.scan(
        local_step, (ones, empty), (block_decay.T, key_state.swapaxes(0, 1))
    )
    (device_decay_back, device_query), (later_decay, later_query) = lax.scan(
        local_step, (ones, empty), (block_decay.T, query_state.swapaxes(0, 1)), reverse=True
    )
    forward_in = prefix((device_decay, device_keys), "seq", combine_states, (ones, empty), False)[1]
    backward_in = prefix(
        (device_decay_back, device_query), "seq", combine_states, (ones, empty), True
    )[1]
    state_before = (
        (prior_decay[:, :, None, None] * forward_in[None] + prior_keys)
        .swapaxes(0, 1)
        .astype(jnp.bfloat16)
    )
    state_after = (
        (later_decay[:, :, None, None] * backward_in[None] + later_query)
        .swapaxes(0, 1)
        .astype(jnp.bfloat16)
    )
    query_key = (
        jnp.einsum("hbte,hbse->hbts", queries_b, keys_b, preferred_element_type=jnp.float32)
        * pair_weight
    ).astype(jnp.bfloat16)
    value_score = (
        jnp.einsum("hbtf,hbsf->hbts", upstream, values_b, preferred_element_type=jnp.float32)
        * pair_weight
    ).astype(jnp.bfloat16)
    query_gradient = jnp.einsum(
        "hbts,hbse->hbte", value_score, keys_b, preferred_element_type=jnp.float32
    ) + from_start[..., None] * jnp.einsum(
        "hbtf,hbef->hbte", upstream, state_before, preferred_element_type=jnp.float32
    )
    key_gradient = jnp.einsum(
        "hbts,hbte->hbse", value_score, queries_b, preferred_element_type=jnp.float32
    ) + to_end[..., None] * jnp.einsum(
        "hbsf,hbef->hbse", values_b, state_after, preferred_element_type=jnp.float32
    )
    value_gradient = jnp.einsum(
        "hbts,hbtf->hbsf", query_key, upstream, preferred_element_type=jnp.float32
    ) + to_end[..., None] * jnp.einsum(
        "hbse,hbef->hbsf", keys_b, state_after, preferred_element_type=jnp.float32
    )
    project_gradient = jnp.stack(
        [
            merge_blocks(query_gradient) * silu_slope(projected[:, 0]) * query_scale,
            merge_blocks(key_gradient) * silu_slope(projected[:, 1]),
            merge_blocks(value_gradient),
        ],
        axis=1,
    ).astype(jnp.bfloat16)
    partial_value = jnp.einsum(
        "tkc,dkc->td", project_gradient, weights_all, preferred_element_type=jnp.float32
    )
    input_gradient = lax.psum_scatter(
        partial_value.astype(jnp.bfloat16), "head", scatter_dimension=1, tiled=True
    )
    weight_gradient = lax.psum_scatter(
        jnp.einsum(
            "td,tkc->dkc", features, project_gradient, preferred_element_type=jnp.float32
        ).astype(jnp.bfloat16),
        "seq",
        scatter_dimension=0,
        tiled=True,
    )
    return (input_gradient, weight_gradient)


def solution(mesh):
    placed = (P("seq", "head"), P("seq", None, "head"), P("seq", "head"), P("head", "seq"), P())
    return jax.shard_map(
        body,
        mesh=mesh,
        in_specs=placed,
        out_specs=(P("seq", "head"), P("seq", None, "head")),
        check_vma=False,
    )
```

profile of v0, /device:TPU:0, one launch (start us, length us, event | category | flops | bytes accessed | tf_op | source)
XLA Modules:
  0.0 778.4 jit_solution(1221711399798025846)
XLA Ops:
  8.8 4.8 reduce-window.6
  19.3 109.7 %all-gather.7.cloned.1.call-done = bf16[1024,6144]{1,0:T(8,128)(2,1)} async-done(((bf16[1024,768]{1,0:T(8,128)(2,1)}), bf16[1024,6144]{1,0:T(8,128)(2,1)}) %all-gather.7.cloned.1.call-update) | async-done | bytes 12582928 | tf_op jit(solution)/shard_map/all_gather | solution.py:63
  129.1 175.4 %all-gather.9.cloned.1.call-done = bf16[6144,3,512]{2,0,1:T(8,128)(2,1)} async-done(((bf16[1536,3,512]{2,0,1:T(8,128)(2,1)}), bf16[6144,3,512]{2,0,1:T(8,128)(2,1)}) %all-gather.9.cloned.1.call-update) | async-done | bytes 18874384 | tf_op jit(solution)/shard_map/all_gather | solution.py:64
  304.5 23.7 %fusion.9 = f32[1024,3,512]{2,0,1:T(8,128)S(1)} fusion(bf16[6144,3,512]{2,0,1:T(8,128)(2,1)} %all-gather.9.cloned.1.call-done, bf16[1024,6144]{1,0:T(8,128)(2,1)} %all-gather.7.cloned.1.call-done), kind=kOutput, calls=%fused_computation.23 | convolution fusion | flops 19327352832 | bytes 37748736 | tf_op jit(solution)/shard_map/td,dkc->tkc/dot_general | solution.py:65
  336.4 3.0 squeeze.59
  339.5 3.9 convolution_bitcast_fusion
  343.5 4.6 while.70
  350.4 5.5 fusion.16
  355.9 3.7 fusion.11
  363.2 7.5 while.68
  370.7 4.5 fusion.20
  375.6 3.7 fusion.26
  379.3 8.9 %all-reduce.2 = (bf16[16]{0:T(256)(128)(2,1)S(1)}, bf16[16]{0:T(256)(128)(2,1)S(1)}) all-reduce(bf16[16]{0:T(256)(128)(2,1)S(1)} %dynamic-update-slice.1, bf16[16]{0:T(256)(128)(2,1)S(1)} %dynamic-update-slice), channel_id=4, replica_groups=mesh['seq'=4,'head'=8] {'seq'}, use_global_device_ids=true, to_apply=%add.1 | all-reduce | flops 32 | bytes 128
  388.3 11.3 %all-gather.3 = bf16[16,128,128]{2,1,0:T(8,128)(2,1)} all-gather(bf16[4,128,128]{2,1,0:T(8,128)(2,1)S(1)} %convert_element_type.142), channel_id=5, replica_groups=mesh['seq'=4,'head'=8] {'seq'}, dimensions={0}, use_global_device_ids=true | all-gather | bytes 655360 | tf_op jit(solution)/shard_map/all_gather | solution.py:13
  399.6 4.2 while.71
  408.4 9.3 %all-gather.1 = bf16[16,128,128]{2,1,0:T(8,128)(2,1)S(1)} all-gather(bf16[4,128,128]{2,1,0:T(8,128)(2,1)S(1)} %convert_element_type.135), channel_id=3, replica_groups=mesh['seq'=4,'head'=8] {'seq'}, dimensions={0}, use_global_device_ids=true | all-gather | bytes 655360 | tf_op jit(solution)/shard_map/all_gather | solution.py:13
  423.7 3.1 reshape.184
  431.6 3.2 reshape.185
  434.8 4.4 multiply_convert_fusion.4
  440.2 28.6 %convert_bitcast_fusion = bf16[6144,3,512]{0,2,1:T(8,128)(2,1)} fusion(bf16[1024,6144]{1,0:T(8,128)(2,1)} %all-gather.7.cloned.1.call-done, bf16[1024,1,512]{2,0,1:T(8,128)(2,1)S(1)} %copy-done.9, bf16[1024,1,512]{2,0,1:T(8,128)(2,1)S(1)} %get-tuple-element.645, bf16[1024,1,512]{2,0,1:T(8,128)(2,1)S(1)} %get-tuple-element.644), kind=kOutput, calls=%fused_computation.21 | convolution fusion | flops 19339935744 | bytes 34603008 | tf_op jit(solution)/shard_map/td,tkc->dkc/dot_general | solution.py:162
  470.3 24.9 %bitcast_convert_fusion.2 = bf16[1024,6144]{1,0:T(8,128)(2,1)} fusion(bf16[6144,3,512]{2,0,1:T(8,128)(2,1)} %all-gather.9.cloned.1.call-done, bf16[1024,1,512]{2,0,1:T(8,128)(2,1)S(1)} %copy-done.10, bf16[1024,1,512]{2,0,1:T(8,128)(2,1)S(1)} %copy-done.7, bf16[1024,1,512]{2,0,1:T(8,128)(2,1)S(1)} %get-tuple-element.644), kind=kOutput, calls=%fused_computation.20 | convolution fusion | flops 19336790016 | bytes 34603008 | tf_op jit(solution)/shard_map/tkc,dkc->td/dot_general | solution.py:155
  495.3 144.5 %reduce-scatter.5.cloned.1.call-done = bf16[1536,3,512]{0,2,1:T(8,128)(2,1)} async-done(((bf16[6144,3,512]{0,2,1:T(8,128)(2,1)}), bf16[1536,3,512]{0,2,1:T(8,128)(2,1)}) %reduce-scatter.5.cloned.1.call-update) | async-done | bytes 4718608 | tf_op jit(solution)/shard_map/reduce_scatter | solution.py:161
  639.8 6.6 copy.174
  646.4 125.4 %reduce-scatter.3.cloned.1.call-done = bf16[1024,768]{1,0:T(8,128)(2,1)} async-done(((bf16[1024,6144]{1,0:T(8,128)(2,1)}), bf16[1024,768]{1,0:T(8,128)(2,1)}) %reduce-scatter.3.cloned.1.call-update) | async-done | bytes 1572880 | tf_op jit(solution)/shard_map/reduce_scatter | solution.py:158
  (149 shorter events, 55.2 us)
Async XLA Ops:
  7.2 121.9 %all-gather.7.cloned.1.call-start = ((), (), s32[]{:S(2)}) async-start(), calls=%async_computation.2 | async-start | bytes 14155776 | tf_op jit(solution)/shard_map/all_gather | solution.py:63
  7.9 0.9 copy-start.11
  7.9 6.2 copy-start.12
  7.9 6.3 copy-start.8
  7.9 296.5 %all-gather.9.cloned.1.call-start = ((), (), s32[]{:S(2)}) async-start(), calls=%async_computation.3 | async-start | bytes 23592960 | tf_op jit(solution)/shard_map/all_gather | solution.py:64
  8.7 631.1 %reduce-scatter.5.cloned.1.call-start = ((), (), s32[]{:S(2)}) async-start(), calls=%async_computation.5 | async-start | bytes 23592960 | tf_op jit(solution)/shard_map/reduce_scatter | solution.py:161
  15.4 2.4 copy-start.13
  328.2 3.2 copy-start
  336.4 3.0 copy-start.4
  348.1 1.0 copy-start.1
  408.4 10.0 %copy-start.5 = (bf16[4,256,4,128]{3,2,1,0:T(4,128)(2,1)S(1)}, bf16[4,256,4,128]{3,2,1,0:T(4,128)(2,1)}, u32[]{:S(2)}) copy-start(bf16[4,256,4,128]{3,2,1,0:T(4,128)(2,1)} %reshape.181) | copy-start | bytes 3145732
  423.7 3.1 copy-start.2
  431.6 3.2 copy-start.3
  434.8 5.4 copy-start.9
  439.3 1.0 copy-start.6
  468.8 1.2 copy-start.7
  468.8 1.5 copy-start.10
  468.8 303.0 %reduce-scatter.3.cloned.1.call-start = ((), (), s32[]{:S(2)}) async-start(), calls=%async_computation.4 | async-start | bytes 14155776 | tf_op jit(solution)/shard_map/reduce_scatter | solution.py:158
Sparse Core Ops, SparseCore 0:
  9.6 119.4 all-gather.6
  130.9 173.4 all-gather.8
  468.9 170.7 reduce-scatter.4
  642.6 129.1 reduce-scatter.2
where the time goes:
time: 779 us; the launch traced here: 778 us
  waiting for transfers between devices  557 us (72%)
  matrix products  108 us (14%)
  local copies, waits for them, and re-layouts  40 us (5%)
  blocking collectives  29.5 us (4%)
  other arithmetic  28.8 us (4%)
  between operations  14.8 us (2%)
    all_gather x1, waiting for transfers between devices, body(): weights_all = lax.all_gather(projection, 'seq', axis=0, tiled=True)  175 us
    reduce_scatter x1, waiting for transfers between devices, body(): lax.psum_scatter(jnp.einsum('td,tkc->dkc', features, project_gradient, pr...  145 us
    reduce_scatter x1, waiting for transfers between devices, body(): lax.psum_scatter(partial_value.astype(jnp.bfloat16), 'head', scatter_dime...  125 us
    all_gather x1, waiting for transfers between devices, body(): features = lax.all_gather(inputs, 'head', axis=1, tiled=True)  110 us
    dot_general x1, matrix products, body(): jnp.einsum('td,tkc->dkc', features, project_gradient, preferred_element_t...  28.6 us
    dot_general x1, matrix products, body(): jnp.einsum('tkc,dkc->td', project_gradient, weights_all, preferred_elemen...  24.9 us
    dot_general x1, matrix products, body(): jnp.einsum('td,dkc->tkc', features, weights_all, preferred_element_type=j...  23.7 us
    all_gather x2, blocking collectives, prefix(): lax.all_gather(part.astype(kind), axis)  20.6 us
  transfers between devices with their start and end apart: 4, of which 4 were waited for; matrix products, arithmetic and copies ran while one was open for 5% of the time, Pallas kernels for 0%

commit v1 on v0

--- a/solution.py
+++ b/solution.py
@@ -61,7 +61,33 @@
     blocks = tokens // BLOCK
     query_scale = HEAD_DIM ** (-0.5)
     features = lax.all_gather(inputs, "head", axis=1, tiled=True)
-    weights_all = lax.all_gather(projection, "seq", axis=0, tiled=True)
+    passed = lax.axis_size("seq")
+    u1 = lax.axis_index("seq")
+    block_now, q_next, known = (passed, u1, projection.shape[0])
+    weights_all = lax.dynamic_update_slice_in_dim(
+        jnp.zeros(
+            [to_i * block_now if no == 0 else to_i for no, to_i in enumerate(projection.shape)],
+            projection.dtype,
+        ),
+        projection,
+        q_next * known,
+        axis=0,
+    )
+    p_next = tall = projection
+    for p in range(1, block_now // 2 + 1):
+        p_next = lax.ppermute(
+            p_next, axis_name="seq", perm=[(no, (no + 1) % block_now) for no in range(block_now)]
+        )
+        weights_all = lax.dynamic_update_slice_in_dim(
+            weights_all, p_next, (q_next - p) % block_now * known, axis=0
+        )
+        if 2 * p < block_now:
+            tall = lax.ppermute(
+                tall, axis_name="seq", perm=[(no, (no - 1) % block_now) for no in range(block_now)]
+            )
+            weights_all = lax.dynamic_update_slice_in_dim(
+                weights_all, tall, (q_next + p) % block_now * known, axis=0
+            )
     projected = jnp.einsum("td,dkc->tkc", features, weights_all, preferred_element_type=jnp.float32)
     queries = (jax.nn.silu(projected[:, 0]) * query_scale).astype(jnp.bfloat16)
     keys = jax.nn.silu(projected[:, 1]).astype(jnp.bfloat16)

time: 779 us -> 824 us (1.058); the launches traced: 778 us -> 814 us
  local copies, waits for them, and re-layouts: 40 us -> 77.2 us
  waiting for transfers between devices: 557 us -> 542 us
    ppermute x0 -> x3, waiting for transfers between devices: none -> 272 us  [the longest x2 198 us: body(): lax.ppermute(p_next, axis_name='seq', perm=[(no, (no + 1) % block_now) fo...]
    all_gather x1 -> x0, waiting for transfers between devices: 175 us -> none  [body(): weights_all = lax.all_gather(projection, 'seq', axis=0, tiled=True)]
    all_gather x1, waiting for transfers between devices: 110 us -> 0.01 us  [body(): features = lax.all_gather(inputs, 'head', axis=1, tiled=True)]
    dynamic_update_slice x0 -> x4, local copies, waits for them, and re-layouts: none -> 17 us  [the longest x2 9.63 us: body(): lax.dynamic_update_slice_in_dim(weights_all, p_next, (q_next - p) % block...]
  transfers between devices with their start and end apart: 4 -> 6, of which waited for: 4 -> 5; matrix products, arithmetic and copies ran while one was open for 5% -> 8% of each run, Pallas kernels for 0% -> 0%
where the time goes in v1:
time: 824 us; the launch traced here: 814 us
  waiting for transfers between devices  542 us (66%)
  matrix products  111 us (13%)
  local copies, waits for them, and re-layouts  77.2 us (9%)
  other arithmetic  33 us (4%)
  blocking collectives  29.8 us (4%)
  between operations  15 us (2%)
    ppermute x2, waiting for transfers between devices, body(): lax.ppermute(p_next, axis_name='seq', perm=[(no, (no + 1) % block_now) fo...  198 us
    reduce_scatter x1, waiting for transfers between devices, body(): lax.psum_scatter(jnp.einsum('td,tkc->dkc', features, project_gradient, pr...  144 us
    reduce_scatter x1, waiting for transfers between devices, body(): lax.psum_scatter(partial_value.astype(jnp.bfloat16), 'head', scatter_dime...  126 us
    ppermute x1, waiting for transfers between devices, body(): lax.ppermute(tall, axis_name='seq', perm=[(no, (no - 1) % block_now) for...  74 us
    dot_general x1, matrix products, body(): jnp.einsum('td,tkc->dkc', features, project_gradient, preferred_element_t...  27.9 us
    dot_general x1, matrix products, body(): jnp.einsum('tkc,dkc->td', project_gradient, weights_all, preferred_elemen...  25.5 us
    dot_general x1, matrix products, body(): jnp.einsum('td,dkc->tkc', features, weights_all, preferred_element_type=j...  23.9 us
    all_gather x2, blocking collectives, prefix(): lax.all_gather(part.astype(kind), axis)  20.7 us
  transfers between devices with their start and end apart: 6, of which 5 were waited for; matrix products, arithmetic and copies ran while one was open for 8% of the time, Pallas kernels for 0%

profile of v1, /device:TPU:0, one launch (start us, length us, event | category | flops | bytes accessed | tf_op | source)
XLA Modules:
  0.0 814.1 jit_solution(1649570588284470685)
XLA Ops:
  12.0 102.9 %collective-permute-done = bf16[1536,3,512]{2,0,1:T(8,128)(2,1)} collective-permute-done((bf16[1536,3,512]{2,0,1:T(8,128)(2,1)}, bf16[1536,3,512]{2,0,1:T(8,128)(2,1)}, u32[]{:S(2)}, u32[]{:S(2)}) %collective-permute-start) | collective-permute-done | bytes 4718624 | tf_op jit(solution)/shard_map/ppermute | solution.py:78
  116.7 4.8 reduce-window.6
  127.9 7.2 broadcast_in_dim.89
  137.7 4.8 constant_dynamic-update-slice_fusion.2
  142.5 74.0 %collective-permute-done.1 = bf16[1536,3,512]{2,0,1:T(8,128)(2,1)} collective-permute-done((bf16[1536,3,512]{2,0,1:T(8,128)(2,1)}, bf16[1536,3,512]{2,0,1:T(8,128)(2,1)}, u32[]{:S(2)}, u32[]{:S(2)}) %collective-permute-start.1) | collective-permute-done | bytes 4718624 | tf_op jit(solution)/shard_map/ppermute | solution.py:85
  216.5 4.8 constant_dynamic-update-slice_fusion.1
  221.3 95.0 %collective-permute-done.2 = bf16[1536,3,512]{2,0,1:T(8,128)(2,1)} collective-permute-done((bf16[1536,3,512]{2,0,1:T(8,128)(2,1)}, bf16[1536,3,512]{2,0,1:T(8,128)(2,1)}, u32[]{:S(2)}, u32[]{:S(2)}) %collective-permute-start.2) | collective-permute-done | bytes 4718624 | tf_op jit(solution)/shard_map/ppermute | solution.py:78
  316.3 4.8 constant_dynamic-update-slice_fusion
  321.1 23.9 %fusion.12 = f32[1024,3,512]{0,2,1:T(8,128)S(1)} fusion(bf16[6144,3,512]{2,0,1:T(8,128)(2,1)} %constant_dynamic-update-slice_fusion, bf16[1024,6144]{1,0:T(8,128)(2,1)} %all-gather.6.cloned.1.call-done), kind=kOutput, calls=%fused_computation.30 | convolution fusion | flops 19327352832 | bytes 37748736 | tf_op jit(solution)/shard_map/td,dkc->tkc/dot_general | solution.py:91
  367.1 4.6 while.70
  377.1 5.5 fusion.19
  389.9 7.3 while.68
  397.2 4.4 fusion.23
  405.7 9.1 %all-reduce.2 = (bf16[16]{0:T(256)(128)(2,1)S(1)}, bf16[16]{0:T(256)(128)(2,1)S(1)}) all-reduce(bf16[16]{0:T(256)(128)(2,1)S(1)} %dynamic-update-slice.1, bf16[16]{0:T(256)(128)(2,1)S(1)} %dynamic-update-slice), channel_id=4, replica_groups=mesh['seq'=4,'head'=8] {'seq'}, use_global_device_ids=true, to_apply=%add.1 | all-reduce | flops 32 | bytes 128
  415.0 10.5 %all-gather.3 = bf16[16,128,128]{2,1,0:T(8,128)(2,1)} all-gather(bf16[4,128,128]{2,1,0:T(8,128)(2,1)S(1)} %convert_element_type.142), channel_id=5, replica_groups=mesh['seq'=4,'head'=8] {'seq'}, dimensions={0}, use_global_device_ids=true | all-gather | bytes 655360 | tf_op jit(solution)/shard_map/all_gather | solution.py:13
  425.5 4.2 while.71
  436.2 10.2 %all-gather.1 = bf16[16,128,128]{2,1,0:T(8,128)(2,1)} all-gather(bf16[4,128,128]{2,1,0:T(8,128)(2,1)S(1)} %convert_element_type.135), channel_id=3, replica_groups=mesh['seq'=4,'head'=8] {'seq'}, dimensions={0}, use_global_device_ids=true | all-gather | bytes 655360 | tf_op jit(solution)/shard_map/all_gather | solution.py:13
  446.4 4.4 while.69
  470.2 4.4 multiply_convert_fusion.4
  475.9 27.9 %convert_bitcast_fusion = bf16[6144,3,512]{0,2,1:T(8,128)(2,1)} fusion(bf16[1024,6144]{1,0:T(8,128)(2,1)} %all-gather.6.cloned.1.call-done, bf16[1024,1,512]{0,2,1:T(8,128)(2,1)S(1)} %copy-done.11, bf16[1024,1,512]{0,2,1:T(8,128)(2,1)S(1)} %get-tuple-element.645, bf16[1024,1,512]{0,2,1:T(8,128)(2,1)S(1)} %get-tuple-element.644), kind=kOutput, calls=%fused_computation.21 | convolution fusion | flops 19339935744 | bytes 34603008 | tf_op jit(solution)/shard_map/td,tkc->dkc/dot_general | solution.py:188
  505.4 25.5 %bitcast_convert_fusion.2 = bf16[1024,6144]{1,0:T(8,128)(2,1)} fusion(bf16[6144,3,512]{2,0,1:T(8,128)(2,1)} %constant_dynamic-update-slice_fusion, bf16[1024,1,512]{0,2,1:T(8,128)(2,1)} %stack_reshape.4, bf16[1024,1,512]{0,2,1:T(8,128)(2,1)S(1)} %copy-done.9, bf16[1024,1,512]{0,2,1:T(8,128)(2,1)S(1)} %copy-done.7), kind=kOutput, calls=%fused_computation.20 | convolution fusion | flops 19336790016 | bytes 34603008 | tf_op jit(solution)/shard_map/tkc,dkc->td/dot_general | solution.py:181
  530.9 144.3 %reduce-scatter.5.cloned.1.call-done = bf16[1536,3,512]{0,2,1:T(8,128)(2,1)} async-done(((bf16[6144,3,512]{0,2,1:T(8,128)(2,1)}), bf16[1536,3,512]{0,2,1:T(8,128)(2,1)}) %reduce-scatter.5.cloned.1.call-update) | async-done | bytes 4718608 | tf_op jit(solution)/shard_map/reduce_scatter | solution.py:187
  675.2 6.6 copy.179
  681.8 125.6 %reduce-scatter.3.cloned.1.call-done = bf16[1024,768]{1,0:T(8,128)(2,1)} async-done(((bf16[1024,6144]{1,0:T(8,128)(2,1)}), bf16[1024,768]{1,0:T(8,128)(2,1)}) %reduce-scatter.3.cloned.1.call-update) | async-done | bytes 1572880 | tf_op jit(solution)/shard_map/reduce_scatter | solution.py:184
  (165 shorter events, 102.3 us)
Async XLA Ops:
  7.2 117.0 %copy-start.12 = (s32[4]{0:T(128)S(1)}, s32[4]{0:T(128)}, u32[]{:S(2)}) copy-start(s32[4]{0:T(128)} %param.17) | copy-start | bytes 52
  7.2 115.6 %copy-start.10 = (bf16[1024,512]{1,0:T(8,128)(2,1)S(1)}, bf16[1024,512]{1,0:T(8,128)(2,1)}, u32[]{:S(2)}) copy-start(bf16[1024,512]{1,0:T(8,128)(2,1)} %param.15) | copy-start | bytes 3145732
  7.2 313.9 %all-gather.6.cloned.1.call-start = ((), (), s32[]{:S(2)}) async-start(), calls=%async_computation.2 | async-start | bytes 14155776 | tf_op jit(solution)/shard_map/all_gather | solution.py:63
  7.9 667.2 %reduce-scatter.5.cloned.1.call-start = ((), (), s32[]{:S(2)}) async-start(), calls=%async_computation.4 | async-start | bytes 23592960 | tf_op jit(solution)/shard_map/reduce_scatter | solution.py:187
  8.0 106.9 %collective-permute-start = (bf16[1536,3,512]{2,0,1:T(8,128)(2,1)}, bf16[1536,3,512]{2,0,1:T(8,128)(2,1)}, u32[]{:S(2)}, u32[]{:S(2)}) collective-permute-start(bf16[1536,3,512]{2,0,1:T(8,128)(2,1)} %param.14), channel_id=1, source_target_pairs={{0,8},{8,16},{16,24},{24,0},{1,9},{9,17},{17,25},{25,1},{2,10},{10... | collective-permute-start | bytes 14155784 | tf_op jit(solution)/shard_map/ppermute | solution.py:78
  11.0 205.6 %collective-permute-start.1 = (bf16[1536,3,512]{2,0,1:T(8,128)(2,1)}, bf16[1536,3,512]{2,0,1:T(8,128)(2,1)}, u32[]{:S(2)}, u32[]{:S(2)}) collective-permute-start(bf16[1536,3,512]{2,0,1:T(8,128)(2,1)} %param.14), channel_id=1, source_target_pairs={{0,24},{8,0},{16,8},{24,16},{1,25},{9,1},{17,9},{25,17},{2,26},{10... | collective-permute-start | bytes 14155784 | tf_op jit(solution)/shard_map/ppermute | solution.py:85
  114.9 201.4 %collective-permute-start.2 = (bf16[1536,3,512]{2,0,1:T(8,128)(2,1)}, bf16[1536,3,512]{2,0,1:T(8,128)(2,1)}, u32[]{:S(2)}, u32[]{:S(2)}) collective-permute-start(bf16[1536,3,512]{2,0,1:T(8,128)(2,1)} %collective-permute-done), channel_id=1, source_target_pairs={{0,8},{8,16},{16,24},{24,0},{1,9},{9,17},{17,25},{25,1},{2,10},{10... | collective-permute-start | bytes 14155784 | tf_op jit(solution)/shard_map/ppermute | solution.py:78
  124.2 2.2 copy-start.13
  127.6 7.5 slice-start
  127.9 7.3 slice-start.1
  345.0 3.9 copy-start
  359.6 3.4 copy-start.4
  371.7 1.0 copy-start.1
  436.2 14.6 %copy-start.5 = (bf16[4,256,4,128]{3,2,1,0:T(4,128)(2,1)S(1)}, bf16[4,256,4,128]{3,2,1,0:T(4,128)(2,1)}, u32[]{:S(2)}) copy-start(bf16[4,256,4,128]{3,2,1,0:T(4,128)(2,1)} %reshape.181) | copy-start | bytes 3145732
  457.4 3.4 copy-start.2
  466.7 3.4 copy-start.3
  470.2 5.8 copy-start.11
  474.6 1.0 copy-start.6
  474.6 1.3 copy-start.8
  503.9 1.2 copy-start.7
  503.9 1.5 copy-start.9
  503.9 303.5 %reduce-scatter.3.cloned.1.call-start = ((), (), s32[]{:S(2)}) async-start(), calls=%async_computation.3 | async-start | bytes 14155776 | tf_op jit(solution)/shard_map/reduce_scatter | solution.py:184
Sparse Core Ops, SparseCore 0:
  9.6 119.4 all-gather.5
  504.0 171.1 reduce-scatter.4
  678.2 129.1 reduce-scatter.2
